TPU v7x, 32 devices: a whole 2x2x4 slice. The times are simulated.
32 devices in a mesh: img: 8 (over z, y), pix: 4 (over x, core).
Axes of the slice: x: 2, y: 2, z: 4, core: 2. Of those that a mesh axis runs over, the one named last changes fastest.
Arguments:
- images: bfloat16 [3072, 16384], P('img', 'pix'), may hold values from -12 to 12
- inverse_noise_scale: float32 [3072], P('img'), may hold values from 0.4 to 4
- projections: bfloat16 [8192, 16384], P('img', 'pix'), may hold values from -1 to 1
- group_search_blocks: int32 [8, 16], P('img'), may hold values from 0 to 63, as said below
- search_list_count: int32 [8], P('img'), may hold values from 12 to 16, as said below
Outputs:
- projection_sums: float32 [8192, 16384], P('img', 'pix')
- log_evidence: float32 [3072], P(('img', 'pix'))
Inputs may be any that keep to these rules, and one draw needn't show every extreme that they name: `group_search_blocks`: each row lists 16 different block ids; block b is owned by index b // 8 of img. Among the first search_list_count[g] entries of row g no owner appears more than 2 times, and in every draw one owner has 2 of its blocks among the first 2 entries of every row. `search_list_count`: some group's count is 16 in every draw.
All inputs are finite; a program needn't handle non-finite values.
Results may differ from a plain program's by a relative error of at most 0.004.
Values may be sent and summed in bfloat16 or wider, within the bound.
No kernel may reach another device: no remote copies, remote signals or barrier semaphores. Data moves between devices by JAX's collectives and lax.ppermute only.
A program may use at most 128 MiB of HBM per device.

v0:
```python
import jax
import jax.numpy as jnp
from jax import lax
from jax.sharding import PartitionSpec as P

BLOCK = 128
CAP = 2
MAXL = 16


def normalise(totals, scaling, slot_used):
    logits = totals * scaling[None, :, None, None]
    live_mask = slot_used[:, None, :, None]
    logits = jnp.where(live_mask, logits, jnp.float32(-1e30))
    row_peak = jnp.max(logits, axis=(0, 2, 3), keepdims=True)
    exponent = jnp.where(live_mask, jnp.exp(logits - row_peak), jnp.float32(0.0))
    row_total = jnp.sum(exponent, axis=(0, 2, 3), keepdims=True)
    weights = (exponent / row_total).astype(jnp.bfloat16)
    marginal_likelihood = (row_peak + jnp.log(row_total)).reshape(-1)
    return (weights, marginal_likelihood)


def on_device(images, inverse_noise_scale, projections, group_search_blocks, search_list_count):
    group_rows, pixels = images.shape
    n_groups = lax.axis_size("img")
    n_shares = lax.axis_size("pix")
    owned_blocks = projections.shape[0] // BLOCK
    every_list, every_count = (
        lax.all_gather(group_search_blocks, "img", axis=0, tiled=True),
        lax.all_gather(search_list_count, "img", axis=0, tiled=True),
    )
    own_index = lax.axis_index("img")
    positions = jnp.arange(MAXL, dtype=jnp.int32)
    slot_ids = jnp.arange(CAP, dtype=jnp.int32)
    live_entry = positions[None, :] < every_count[:, None]
    local_hit = live_entry & (every_list // owned_blocks == own_index)
    slot_rank = jnp.cumsum(local_hit.astype(jnp.int32), axis=1) - 1
    slot_pick = local_hit[:, None, :] & (slot_rank[:, None, :] == slot_ids[None, :, None])
    slot_offset = jnp.sum(jnp.where(slot_pick, every_list[:, None, :] % owned_blocks, 0), axis=2)
    slot_filled = jnp.any(slot_pick, axis=2)
    own_live = positions < search_list_count[0]
    own_owner = group_search_blocks[0] // owned_blocks
    per_owner = jnp.sum(
        (
            own_live[None, :]
            & (own_owner[None, :] == jnp.arange(n_groups, dtype=jnp.int32)[:, None])
        ).astype(jnp.int32),
        axis=1,
    )
    slot_used = slot_ids[None, :] < per_owner[:, None]
    stacked = projections.reshape(owned_blocks, BLOCK, pixels)
    outgoing = jnp.take(stacked, slot_offset.reshape(-1), axis=0).reshape(
        n_groups, CAP, BLOCK, pixels
    )
    everyone = lax.all_gather(images, "img", axis=0, tiled=True).reshape(
        n_groups, group_rows, pixels
    )
    local_scores = jnp.einsum(
        "gcrf,gif->gicr", outgoing, everyone, preferred_element_type=jnp.float32
    )
    partial_value = lax.all_to_all(local_scores, "img", split_axis=0, concat_axis=0, tiled=True)
    share_rows = group_rows // n_shares
    first_row = lax.axis_index("pix") * share_rows
    totals = lax.psum(partial_value, "pix")
    weights, marginal_likelihood = normalise(totals, inverse_noise_scale, slot_used)
    evidence_out = lax.dynamic_slice_in_dim(marginal_likelihood, first_row, share_rows)
    weights_home = lax.all_to_all(weights, "img", split_axis=0, concat_axis=0, tiled=True)
    arriving = jnp.einsum(
        "gicr,gif->gcrf", weights_home, everyone, preferred_element_type=jnp.float32
    ).astype(jnp.bfloat16)
    placement = (
        slot_offset.reshape(-1)[None, :] == jnp.arange(owned_blocks, dtype=jnp.int32)[:, None]
    ) & slot_filled.reshape(-1)[None, :]
    placement_table = placement.astype(jnp.bfloat16)
    running_total = jnp.dot(
        placement_table,
        arriving.reshape(n_groups * CAP, BLOCK * pixels),
        preferred_element_type=jnp.float32,
    )
    return (running_total.reshape(owned_blocks * BLOCK, pixels), evidence_out)


def solution(mesh):
    placed = (P("img", "pix"), P("img"), P("img", "pix"), P("img", None), P("img"))
    return jax.shard_map(
        on_device,
        mesh=mesh,
        in_specs=placed,
        out_specs=(P("img", "pix"), P(("img", "pix"))),
        check_vma=False,
    )
```

profile of v0, /device:TPU:0, one launch (start us, length us, event | category | flops | bytes accessed | tf_op | source)
XLA Modules:
  0.0 769.8 jit_solution(3247662707351451047)
XLA Ops:
  7.2 0.0 copy-start.3
  7.2 0.0 copy-start.2
  7.2 0.0 all-gather.3.cloned.1.call-start
  7.2 0.7 all-gather.3.cloned.1.call-update
  7.9 0.0 all-reduce.3.cloned.1.call-start
  8.6 0.0 copy-done.3
  8.6 0.6 dynamic-slice.2
  9.2 0.8 dynamic-update-slice
  10.0 13.3 %all-reduce = s32[8]{0:T(128)S(1)} all-reduce(s32[8]{0:T(128)S(1)} %dynamic-update-slice), channel_id=1, replica_groups=mesh['img'=8,'pix'=4] {'img'}, use_global_device_ids=true, to_apply=%add | all-reduce | flops 8 | bytes 64
  23.3 0.0 copy-done.2
  23.3 43.3 %all-gather = s32[8,1,16]{2,1,0:T(1,128)S(1)} all-gather(s32[1,1,16]{2,1,0:T(1,128)S(1)} %bitcast.33), channel_id=1, replica_groups=mesh['img'=8,'pix'=4] {'img'}, dimensions={0}, use_global_device_ids=true | all-gather | bytes 576 | tf_op jit(solution)/shard_map/all_gather | solution.py:29
  66.6 0.1 fusion.24
  66.6 0.2 reduce_window_sum.11
  66.8 0.1 select_reduce_fusion
  67.0 0.1 copy.7
  67.1 0.1 copy.9
  67.2 0.1 reshape.124
  67.3 10.7 %gather_fusion = bf16[16,128,4096]{2,1,0:T(8,128)(2,1)} fusion(bf16[8,128,4096]{2,1,0:T(8,128)(2,1)} %bitcast.27, s32[1024]{0:T(1024)S(1)} %pad_clamp_fusion), kind=kCustom, calls=%fused_computation | custom fusion | bytes 33554496 | tf_op jit(solution)/shard_map/jit(_take)/gather | solution.py:52
  78.0 414.8 %all-gather.3.cloned.1.call-done = bf16[3072,4096]{1,0:T(8,128)(2,1)} async-done(((bf16[384,4096]{1,0:T(8,128)(2,1)}), bf16[3072,4096]{1,0:T(8,128)(2,1)}) %all-gather.3.cloned.1.call-update) | async-done | bytes 25165840 | tf_op jit(solution)/shard_map/all_gather | solution.py:55
  492.7 21.4 %fusion.6 = f32[8,384,2,128]{1,3,2,0:T(8,128)S(1)} fusion(bf16[8,384,4096,1]{2,1,3,0:T(8,128)(2,1)} %bitcast.28, bf16[8,2,128,4096]{3,2,1,0:T(8,128)(2,1)} %bitcast.30, pred[8,2]{1,0:T(8,128)(4,1)S(1)} %copy.9), kind=kOutput, calls=%fused_computation.11 | convolution fusion | flops 6450839552 | bytes 45088784 | tf_op jit(solution)/shard_map/gcrf,gif->gicr/dot_general | solution.py:58
  514.2 75.3 %all_to_all.10 = f32[8,384,2,128]{1,3,2,0:T(8,128)} all-to-all(f32[8,384,2,128]{1,3,2,0:T(8,128)S(1)} %fusion.6), channel_id=1, replica_groups=mesh['img'=8,'pix'=4] {'img'}, dimensions={0} | all-to-all | bytes 6291456 | tf_op jit(solution)/shard_map/all_to_all | solution.py:61
  589.5 0.0 copy-start.1
  589.5 0.0 all-reduce.3.cloned.1.call-update
  589.6 0.1 convert_reduce_fusion
  589.7 0.1 iota_compare_fusion.2
  589.8 67.4 %all-reduce.3.cloned.1.call-done = f32[8,384,2,128]{1,3,2,0:T(8,128)} async-done(((f32[8,384,2,128]{1,3,2,0:T(8,128)}), f32[8,384,2,128]{1,3,2,0:T(8,128)}) %all-reduce.3.cloned.1.call-update) | async-done | bytes 3145744 | tf_op jit(solution)/shard_map/psum | solution.py:64
  657.1 0.0 copy-done.1
  657.1 0.0 copy-start
  657.1 2.5 fusion.4
  659.7 0.3 copy-done
  660.0 0.8 fusion.5
  660.8 2.0 divide_convert_fusion
  662.8 5.5 all-to-all-start.1
  668.3 0.1 eq.56
  668.4 0.1 fusion.10
  668.6 0.1 copy.8
  668.7 0.1 and.62
  668.8 0.6 dynamic_slice.3
  669.4 35.7 %all-to-all-done.1 = bf16[8,384,2,128]{1,3,2,0:T(8,128)(2,1)S(1)} async-done(((bf16[8,384,2,128]{1,3,2,0:T(8,128)(2,1)}), bf16[8,384,2,128]{1,3,2,0:T(8,128)(2,1)S(1)}, u32[]{:S(2)}, u32[]{:S(2)}) %all-to-all-start.1) | async-done | bytes 1572896 | tf_op jit(solution)/shard_map/all_to_all | solution.py:67
  705.1 21.3 %convolution_convert_fusion = bf16[8,2,128,4096]{3,2,1,0:T(8,128)(2,1)} fusion(bf16[8,384,2,128]{1,3,2,0:T(8,128)(2,1)S(1)} %all-to-all-done.1, bf16[8,384,4096,1]{2,1,3,0:T(8,128)(2,1)} %bitcast.29), kind=kOutput, calls=%fused_computation.4 | convolution fusion | flops 6450839552 | bytes 43515904 | tf_op jit(solution)/shard_map/gicr,gif->gcrf/dot_general | solution.py:68
  726.3 14.8 %copy.12 = bf16[2,8,128,4096]{3,1,2,0:T(8,128)(2,1)S(1)} copy(bf16[2,8,128,4096]{3,2,1,0:T(8,128)(2,1)} %bitcast.26) | data formatting | bytes 33554432
  741.1 7.0 fusion.15
  748.1 14.9 %reshape.127 = f32[1024,4096]{1,0:T(8,128)} reshape(f32[8,524288]{1,0:T(8,128)} %fusion.15) | data formatting | bytes 33554432 | tf_op jit(solution)/shard_map/reshape | solution.py:80
  (9 shorter events, 0.1 us)
Async XLA Ops:
  7.2 1.5 copy-start.3
  7.2 16.1 %copy-start.2 = (s32[1,16]{1,0:T(1,128)S(1)}, s32[1,16]{1,0:T(1,128)}, u32[]{:S(2)}) copy-start(s32[1,16]{1,0:T(1,128)} %param.8) | copy-start | bytes 196
  7.2 485.5 %all-gather.3.cloned.1.call-start = ((), (), s32[]{:S(2)}) async-start(), calls=%async_computation.2 | async-start | bytes 28311552 | tf_op jit(solution)/shard_map/all_gather | solution.py:55
  7.9 649.2 %all-reduce.3.cloned.1.call-start = ((), (), s32[]{:S(2)}) async-start(), calls=%async_computation.3 | async-start | bytes 6291456 | tf_op jit(solution)/shard_map/psum | solution.py:64
  589.5 67.6 %copy-start.1 = (f32[384]{0:T(512)S(1)}, f32[384]{0:T(512)}, u32[]{:S(2)}) copy-start(f32[384]{0:T(512)} %param.6) | copy-start | bytes 4612
  657.1 2.8 copy-start
  662.8 42.2 %all-to-all-start.1 = ((bf16[8,384,2,128]{1,3,2,0:T(8,128)(2,1)}), bf16[8,384,2,128]{1,3,2,0:T(8,128)(2,1)S(1)}, u32[]{:S(2)}, u32[]{:S(2)}) async-start(bf16[8,384,2,128]{1,3,2,0:T(8,128)(2,1)} %divide_convert_fusion), calls=%async_computation.1 | async-start | bytes 3145728 | tf_op jit(solution)/shard_map/all_to_all | solution.py:67
Sparse Core Ops, SparseCore 0:
  9.5 483.1 all-gather.2
  589.7 67.4 all-reduce.2
where the time goes:
time: 770 us
  waiting for transfers between devices  519 us (67%)
  blocking collectives  132 us (17%)
  matrix products  49.7 us (6%)
  local copies, waits for them, and re-layouts  43.1 us (6%)
  between operations  14.8 us (2%)
    all_gather x1, waiting for transfers between devices, on_device(): lax.all_gather(images, 'img', axis=0, tiled=True)  415 us
    all_to_all x1, blocking collectives, on_device(): lax.all_to_all(local_scores, 'img', split_axis=0, concat_axis=0, tiled=True)  75.3 us
    psum x1, waiting for transfers between devices, on_device(): totals = lax.psum(partial_value, 'pix')  67.4 us
    all_gather x1, blocking collectives, on_device(): lax.all_gather(group_search_blocks, 'img', axis=0, tiled=True)  43.3 us
    all_to_all x1, waiting for transfers between devices, on_device(): lax.all_to_all(weights, 'img', split_axis=0, concat_axis=0, tiled=True)  35.7 us
    dot_general x1, matrix products, on_device(): jnp.einsum('gcrf,gif->gicr', outgoing, everyone, preferred_element_type=j...  21.4 us
    dot_general x1, matrix products, on_device(): jnp.einsum('gicr,gif->gcrf', weights_home, everyone, preferred_element_ty...  21.3 us
    unnamed x12, local copies, waits for them, and re-layouts  16.4 us
  transfers between devices with their start and end apart: 3, of which 3 were waited for; matrix products, arithmetic and copies ran while one was open for 2% of the time, Pallas kernels for 0%

commit v1 on v0

--- a/solution.py
+++ b/solution.py
@@ -61,7 +61,7 @@
     partial_value = lax.all_to_all(local_scores, "img", split_axis=0, concat_axis=0, tiled=True)
     share_rows = group_rows // n_shares
     first_row = lax.axis_index("pix") * share_rows
-    totals = lax.psum(partial_value, "pix")
+    totals = jnp.sum(lax.all_gather(partial_value, "pix"), axis=0)
     weights, marginal_likelihood = normalise(totals, inverse_noise_scale, slot_used)
     evidence_out = lax.dynamic_slice_in_dim(marginal_likelihood, first_row, share_rows)
     weights_home = lax.all_to_all(weights, "img", split_axis=0, concat_axis=0, tiled=True)

time: 770 us -> 792 us (1.029)
  waiting for transfers between devices: 519 us -> 533 us
    all_gather x0 -> x1, waiting for transfers between devices: none -> 81 us  [on_device(): totals = jnp.sum(lax.all_gather(partial_value, 'pix'), axis=0)]
    psum x1 -> x0, waiting for transfers between devices: 67.4 us -> none  [on_device(): totals = lax.psum(partial_value, 'pix')]
    unnamed x12 -> x10, local copies, waits for them, and re-layouts: 16.4 us -> 16.1 us
where the time goes in v1:
time: 792 us; the launch traced here: 791 us
  waiting for transfers between devices  533 us (67%)
  blocking collectives  132 us (17%)
  local copies, waits for them, and re-layouts  47.6 us (6%)
  matrix products  46.9 us (6%)
  between operations  14.8 us (2%)
  other arithmetic  11.6 us (1%)
    all_gather x1, waiting for transfers between devices, on_device(): lax.all_gather(images, 'img', axis=0, tiled=True)  415 us
    all_gather x1, waiting for transfers between devices, on_device(): totals = jnp.sum(lax.all_gather(partial_value, 'pix'), axis=0)  81 us
    all_to_all x1, blocking collectives, on_device(): lax.all_to_all(local_scores, 'img', split_axis=0, concat_axis=0, tiled=True)  75.4 us
    all_gather x1, blocking collectives, on_device(): lax.all_gather(group_search_blocks, 'img', axis=0, tiled=True)  43.3 us
    all_to_all x1, waiting for transfers between devices, on_device(): lax.all_to_all(weights, 'img', split_axis=0, concat_axis=0, tiled=True)  36.4 us
    dot_general x1, matrix products, on_device(): jnp.einsum('gicr,gif->gcrf', weights_home, everyone, preferred_element_ty...  21.3 us
    dot_general x1, matrix products, on_device(): jnp.einsum('gcrf,gif->gicr', outgoing, everyone, preferred_element_type=j...  18.7 us
    unnamed x10, local copies, waits for them, and re-layouts  16.1 us
  transfers between devices with their start and end apart: 3, of which 3 were waited for; matrix products, arithmetic and copies ran while one was open for 2% of the time, Pallas kernels for 0%

profile of v1, /device:TPU:0, one launch (start us, length us, event | category | flops | bytes accessed | tf_op | source)
XLA Modules:
  0.0 791.4 jit_solution(3262616589814463363)
XLA Ops:
  7.2 0.0 copy-start.2
  7.2 0.0 copy-start.1
  7.2 0.0 all-gather.5.cloned.1.call-start
  7.2 0.7 all-gather.5.cloned.1.call-update
  7.9 0.0 all-gather.7.cloned.1.call-start
  8.6 0.0 copy-done.2
  8.6 0.6 dynamic-slice.2
  9.2 0.8 dynamic-update-slice
  10.0 13.3 %all-reduce = s32[8]{0:T(128)S(1)} all-reduce(s32[8]{0:T(128)S(1)} %dynamic-update-slice), channel_id=1, replica_groups=mesh['img'=8,'pix'=4] {'img'}, use_global_device_ids=true, to_apply=%add | all-reduce | flops 8 | bytes 64
  23.3 0.0 copy-done.1
  23.3 43.3 %all-gather.1 = s32[8,1,16]{2,1,0:T(1,128)S(1)} all-gather(s32[1,1,16]{2,1,0:T(1,128)S(1)} %bitcast.35), channel_id=1, replica_groups=mesh['img'=8,'pix'=4] {'img'}, dimensions={0}, use_global_device_ids=true | all-gather | bytes 576 | tf_op jit(solution)/shard_map/all_gather | solution.py:29
  66.6 0.1 fusion.24
  66.6 0.2 reduce_window_sum.11
  66.8 0.1 select_reduce_fusion
  67.0 0.1 copy.10
  67.1 0.1 copy.12
  67.2 0.1 reshape.124
  67.3 10.7 %gather_fusion = bf16[16,128,4096]{2,1,0:T(8,128)(2,1)} fusion(bf16[8,128,4096]{2,1,0:T(8,128)(2,1)} %bitcast.28, s32[1024]{0:T(1024)S(1)} %pad_clamp_fusion), kind=kCustom, calls=%fused_computation | custom fusion | bytes 33554496 | tf_op jit(solution)/shard_map/jit(_take)/gather | solution.py:52
  78.0 414.8 %all-gather.5.cloned.1.call-done = bf16[3072,4096]{1,0:T(8,128)(2,1)} async-done(((bf16[384,4096]{1,0:T(8,128)(2,1)}), bf16[3072,4096]{1,0:T(8,128)(2,1)}) %all-gather.5.cloned.1.call-update) | async-done | bytes 25165840 | tf_op jit(solution)/shard_map/all_gather | solution.py:55
  492.7 18.7 %fusion.6 = f32[8,384,2,128]{1,3,2,0:T(8,128)} fusion(bf16[8,384,4096,1]{2,1,3,0:T(8,128)(2,1)} %bitcast.29, bf16[8,2,128,4096]{3,2,1,0:T(8,128)(2,1)} %bitcast.31, pred[8,2]{1,0:T(8,128)(4,1)S(1)} %copy.12), kind=kOutput, calls=%fused_computation.11 | convolution fusion | flops 6450839552 | bytes 45088784 | tf_op jit(solution)/shard_map/gcrf,gif->gicr/dot_general | solution.py:58
  511.4 75.4 %all_to_all.10 = f32[8,384,2,128]{1,3,2,0:T(8,128)S(1)} all-to-all(f32[8,384,2,128]{1,3,2,0:T(8,128)} %fusion.6), channel_id=1, replica_groups=mesh['img'=8,'pix'=4] {'img'}, dimensions={0} | all-to-all | bytes 6291456 | tf_op jit(solution)/shard_map/all_to_all | solution.py:61
  586.8 2.4 copy.14
  589.2 0.0 all-gather.7.cloned.1.call-update
  589.2 0.1 convert_reduce_fusion
  589.4 0.1 iota_compare_fusion.2
  589.4 81.0 %all-gather.7.cloned.1.call-done = f32[32,384,2,128]{3,1,2,0:T(8,128)} async-done(((f32[8,384,2,128]{3,1,2,0:T(8,128)}), f32[32,384,2,128]{3,1,2,0:T(8,128)}) %all-gather.7.cloned.1.call-update) | async-done | bytes 12582928 | tf_op jit(solution)/shard_map/all_gather | solution.py:64
  670.5 7.5 reduce_sum.38
  678.0 0.0 copy-start
  678.0 2.4 copy.15
  680.4 0.0 copy-done
  680.4 0.5 fusion.4
  680.9 0.8 fusion.5
  681.7 2.0 divide_convert_fusion
  683.7 5.5 all-to-all-start.1
  689.2 0.1 eq.56
  689.3 0.1 fusion.10
  689.4 0.1 copy.11
  689.5 0.1 and.62
  689.6 0.6 dynamic_slice.3
  690.2 36.4 %all-to-all-done.1 = bf16[8,384,2,128]{1,3,2,0:T(8,128)(2,1)S(1)} async-done(((bf16[8,384,2,128]{1,3,2,0:T(8,128)(2,1)}), bf16[8,384,2,128]{1,3,2,0:T(8,128)(2,1)S(1)}, u32[]{:S(2)}, u32[]{:S(2)}) %all-to-all-start.1) | async-done | bytes 1572896 | tf_op jit(solution)/shard_map/all_to_all | solution.py:67
  726.6 21.3 %convolution_convert_fusion = bf16[8,2,128,4096]{3,2,1,0:T(8,128)(2,1)} fusion(bf16[8,384,2,128]{1,3,2,0:T(8,128)(2,1)S(1)} %all-to-all-done.1, bf16[8,384,4096,1]{2,1,3,0:T(8,128)(2,1)} %bitcast.30), kind=kOutput, calls=%fused_computation.4 | convolution fusion | flops 6450839552 | bytes 43515904 | tf_op jit(solution)/shard_map/gicr,gif->gcrf/dot_general | solution.py:68
  747.9 14.8 %copy.17 = bf16[2,8,128,4096]{3,1,2,0:T(8,128)(2,1)S(1)} copy(bf16[2,8,128,4096]{3,2,1,0:T(8,128)(2,1)} %bitcast.27) | data formatting | bytes 33554432
  762.7 7.0 fusion.15
  769.6 14.9 %reshape.127 = f32[1024,4096]{1,0:T(8,128)} reshape(f32[8,524288]{1,0:T(8,128)} %fusion.15) | data formatting | bytes 33554432 | tf_op jit(solution)/shard_map/reshape | solution.py:80
  (9 shorter events, 0.1 us)
Async XLA Ops:
  7.2 1.5 copy-start.2
  7.2 16.1 %copy-start.1 = (s32[1,16]{1,0:T(1,128)S(1)}, s32[1,16]{1,0:T(1,128)}, u32[]{:S(2)}) copy-start(s32[1,16]{1,0:T(1,128)} %param.8) | copy-start | bytes 196
  7.2 485.5 %all-gather.5.cloned.1.call-start = ((), (), s32[]{:S(2)}) async-start(), calls=%async_computation.2 | async-start | bytes 28311552 | tf_op jit(solution)/shard_map/all_gather | solution.py:55
  7.9 662.5 %all-gather.7.cloned.1.call-start = ((), (), s32[]{:S(2)}) async-start(), calls=%async_computation.3 | async-start | bytes 15728640 | tf_op jit(solution)/shard_map/all_gather | solution.py:64
  678.0 2.4 copy-start
  683.7 42.9 %all-to-all-start.1 = ((bf16[8,384,2,128]{1,3,2,0:T(8,128)(2,1)}), bf16[8,384,2,128]{1,3,2,0:T(8,128)(2,1)S(1)}, u32[]{:S(2)}, u32[]{:S(2)}) async-start(bf16[8,384,2,128]{1,3,2,0:T(8,128)(2,1)} %divide_convert_fusion), calls=%async_computation.1 | async-start | bytes 3145728 | tf_op jit(solution)/shard_map/all_to_all | solution.py:67
Sparse Core Ops, SparseCore 0:
  9.5 483.1 all-gather.4
  589.3 81.0 all-gather.6
